TPU v7x, 32 devices: a whole 2x2x4 slice. The times are simulated.
32 devices in a mesh: batch: 4 (over y, x), seq: 4 (over z), head: 2 (over core).
Axes of the slice: x: 2, y: 2, z: 4, core: 2. Of those that a mesh axis runs over, the one named last changes fastest.
Arguments:
- hidden: bfloat16 [4, 2048, 1024], P('batch', 'seq', 'head'), may hold values from -6 to 6
- norm_gain: bfloat16 [1024], P('head'), may hold values from 0.099609375 to 1.8984375
- gate_weight: bfloat16 [1024, 2048], P(None, 'head'), may hold values from -0.1875 to 0.1875
- inner_weight: bfloat16 [1024, 2048], P(None, 'head'), may hold values from -0.1875 to 0.1875
- step_weight: bfloat16 [1024, 32], P(None, 'head'), may hold values from -0.375 to 0.375
- maps_weight: bfloat16 [1024, 256], replicated, may hold values from -0.1875 to 0.1875
- inner_kernel: float32 [4, 2048], P(None, 'head'), may hold values from -3 to 3
- inner_bias: float32 [2048], P('head'), may hold values from -1 to 1
- maps_kernel: float32 [4, 256], replicated, may hold values from -3 to 3
- maps_bias: float32 [256], replicated, may hold values from -1 to 1
- step_bias: float32 [32], P('head'), may hold values from -7 to -5
- decay_log: float32 [32], P('head'), may hold values from -5.3 to 1
- skip_gain: float32 [32], P('head'), may hold values from 1 to 4
- gate_gain: float32 [2048], P('head'), may hold values from 0.1 to 1.9
- output_weight: bfloat16 [2048, 1024], P('head'), may hold values from -0.125 to 0.125
- cotangent: bfloat16 [4, 2048, 1024], P('batch', 'seq', 'head'), may hold values from -6 to 6
Outputs:
- output: float32 [4, 2048, 1024], P('batch', 'seq', 'head')
- grad_hidden: float32 [4, 2048, 1024], P('batch', 'seq', 'head')
- grad_norm_gain: float32 [1024], P('head')
- grad_gate_weight: float32 [1024, 2048], P(None, 'head')
- grad_inner_weight: float32 [1024, 2048], P(None, 'head')
- grad_step_weight: float32 [1024, 32], P(None, 'head')
- grad_maps_weight: float32 [1024, 256], replicated
- grad_inner_kernel: float32 [4, 2048], P(None, 'head')
- grad_inner_bias: float32 [2048], P('head')
- grad_maps_kernel: float32 [4, 256], replicated
- grad_maps_bias: float32 [256], replicated
- grad_step_bias: float32 [32], P('head')
- grad_decay_log: float32 [32], P('head')
- grad_skip_gain: float32 [32], P('head')
- grad_gate_gain: float32 [2048], P('head')
- grad_output_weight: float32 [2048, 1024], P('head')
All inputs are finite; a program needn't handle non-finite values.
Results may differ from a plain program's by a relative error of at most 0.0089.
Values may be sent and summed in bfloat16 or wider, within the bound.
A program may use at most 192 MiB of HBM per device.

v0:
```python
import jax
import jax.numpy as jnp
from jax import lax
from jax.sharding import PartitionSpec as P

D = 1024
HEADDIM = 64
STATE = 128
CONV = 4
GROUP = 256
DI = 2048


HIGH = lax.Precision.HIGHEST
EPSILON = 1e-05


def shifted(array, axis, by):
    count = lax.axis_size(axis)
    pairs = [(i, i + by) for i in range(count) if 0 <= i + by < count]
    return lax.ppermute(array, axis, pairs)


def entering(array, axis, combine, identity, reverse):
    count, index = (lax.axis_size(axis), lax.axis_index(axis))
    everything = jax.tree.map(lambda part: lax.all_gather(part, axis), array)
    start = jax.tree.map(
        lambda part, zero: jnp.broadcast_to(jnp.asarray(zero, part.dtype), part.shape),
        array,
        identity,
    )

    def step(k, before):
        at = count - 1 - k if reverse else k
        reached = at > index if reverse else at < index
        new = combine(before, jax.tree.map(lambda part: part[at], everything))
        return jax.tree.map(lambda a, b: jnp.where(reached, a, b), new, before)

    return lax.fori_loop(0, count, step, start)


def silu_slope(values):
    sigmoid = jax.nn.sigmoid(values)
    return sigmoid * (1.0 + values * (1.0 - sigmoid))


def ssd_blocks(inner_act, write_map, read_map, step_size, decay_rates, initial):
    length, heads, headdim = inner_act.shape
    blocks_count = length // GROUP
    inner_blocks = inner_act.reshape(blocks_count, GROUP, heads, headdim)
    write_blocks = write_map.reshape(blocks_count, GROUP, write_map.shape[-1])
    read_blocks = read_map.reshape(blocks_count, GROUP, read_map.shape[-1])
    step_blocks = step_size.reshape(blocks_count, GROUP, heads)
    causal = (jnp.arange(GROUP)[:, None] >= jnp.arange(GROUP)[None, :])[:, :, None]

    def advance(state_in, pieces):
        inner_part, write_part, read_part, step_part = pieces
        cumlog = jnp.cumsum(step_part * decay_rates[None, :], axis=0)
        spread = jnp.where(causal, cumlog[:, None, :] - cumlog[None, :, :], 0.0)
        decays = jnp.where(causal, jnp.exp(spread), 0.0)
        scores = jnp.dot(read_part, write_part.T, precision=HIGH)
        weighted = inner_part * step_part[:, :, None]
        within = jnp.einsum("tsh,shp->thp", decays * scores[:, :, None], weighted, precision=HIGH)
        carried = jnp.einsum("tn,hpn->thp", read_part, state_in, precision=HIGH)
        result = within + jnp.exp(cumlog)[:, :, None] * carried
        remain = jnp.exp(cumlog[-1][None, :] - cumlog)
        fresh = jnp.einsum("shp,sn->hpn", weighted * remain[:, :, None], write_part, precision=HIGH)
        state_out = jnp.exp(cumlog[-1])[:, None, None] * state_in + fresh
        return (state_out, result)

    final, outputs = lax.scan(
        advance, initial, (inner_blocks, write_blocks, read_blocks, step_blocks)
    )
    return (outputs.reshape(length, heads, headdim), final)


def batched_scan(inner_heads, write_map, read_map, step_size, decay_rates, state_in):
    return jax.vmap(ssd_blocks, in_axes=(0, 0, 0, 0, None, 0))(
        inner_heads, write_map, read_map, step_size, decay_rates, state_in
    )


def chain_pair(earlier, later):
    return (earlier[0] * later[0], earlier[1] * later[0][:, :, None, None] + later[1])


def conv_apply(padded, kernel, bias_row, length):
    summed = bias_row
    for offset in range(kernel.shape[0]):
        summed = summed + kernel[offset] * padded[..., offset : offset + length, :]
    return summed


def conv_grads(padded, extended, grad_out, kernel, length):
    leading = tuple(range(grad_out.ndim - 1))
    grad_kernel = jnp.stack(
        [
            jnp.sum(grad_out * padded[..., offset : offset + length, :], axis=leading)
            for offset in range(kernel.shape[0])
        ]
    )
    grad_bias = jnp.sum(grad_out, axis=leading)
    width_less = kernel.shape[0] - 1
    grad_input = jnp.zeros_like(grad_out)
    for offset in range(kernel.shape[0]):
        begin_at = width_less - offset
        grad_input = grad_input + kernel[offset] * extended[..., begin_at : begin_at + length, :]
    return (grad_input, grad_kernel, grad_bias)


def on_device(
    hidden,
    norm_gain,
    gate_weight,
    inner_weight,
    step_weight,
    maps_weight,
    inner_kernel,
    inner_bias,
    maps_kernel,
    maps_bias,
    step_bias,
    decay_log,
    skip_gain,
    gate_gain,
    output_weight,
    cotangent,
):
    seq_count, tok_count, local_width = hidden.shape
    rows_count = seq_count * tok_count
    local_inner = gate_weight.shape[1]
    heads_local = step_weight.shape[1]
    whole_hidden, whole_cotangent, whole_gain = (
        lax.all_gather(hidden, "head", axis=2, tiled=True),
        lax.all_gather(cotangent, "head", axis=2, tiled=True),
        lax.all_gather(norm_gain, "head", axis=0, tiled=True),
    )
    residual = whole_hidden.reshape(rows_count, D).astype(jnp.float32)
    inverse = lax.rsqrt(jnp.mean(residual * residual, axis=-1, keepdims=True) + EPSILON)
    normal = residual * inverse
    normed = (normal * whole_gain.astype(jnp.float32)).astype(jnp.bfloat16)
    gate_pre = jnp.dot(normed, gate_weight, preferred_element_type=jnp.float32)
    inner_pre = jnp.dot(normed, inner_weight, preferred_element_type=jnp.float32)
    maps_pre = jnp.dot(normed, maps_weight, preferred_element_type=jnp.float32)
    step_pre = jnp.dot(normed, step_weight, preferred_element_type=jnp.float32).reshape(
        seq_count, tok_count, heads_local
    )
    inner_seq = inner_pre.reshape(seq_count, tok_count, local_inner)
    maps_seq = maps_pre.reshape(seq_count, tok_count, 2 * STATE)
    edge_inner, edge_maps = shifted(
        (inner_seq[:, tok_count - (CONV - 1) :, :], maps_seq[:, tok_count - (CONV - 1) :, :]),
        "seq",
        1,
    )
    inner_pad = jnp.concatenate([edge_inner, inner_seq], axis=1)
    maps_pad = jnp.concatenate([edge_maps, maps_seq], axis=1)
    inner_conv = conv_apply(inner_pad, inner_kernel, inner_bias, tok_count)
    maps_conv = conv_apply(maps_pad, maps_kernel, maps_bias, tok_count)
    inner_act = jax.nn.silu(inner_conv)
    maps_act = jax.nn.silu(maps_conv)
    write_map = maps_act[..., :STATE]
    read_map = maps_act[..., STATE:]
    step_size = jax.nn.softplus(step_pre + step_bias)
    decay_rates = -jnp.exp(decay_log)
    inner_heads = inner_act.reshape(seq_count, tok_count, heads_local, HEADDIM)
    zero_state = jnp.zeros((seq_count, heads_local, HEADDIM, STATE), jnp.float32)
    local_mix, local_state = batched_scan(
        inner_heads, write_map, read_map, step_size, decay_rates, zero_state
    )
    cumlog = jnp.cumsum(step_size * decay_rates, axis=1)
    total_decay = jnp.exp(cumlog[:, -1, :])
    identity = (jnp.ones_like(total_decay), jnp.zeros_like(local_state))
    prefix_decay, state_in = entering(
        (total_decay, local_state), "seq", chain_pair, identity, False
    )
    carried = jnp.einsum("stn,shpn->sthp", read_map, state_in, precision=HIGH)
    mixed_out = (
        local_mix
        + jnp.exp(cumlog)[..., None] * carried
        + skip_gain[None, None, :, None] * inner_heads
    )
    mixed_flat = mixed_out.reshape(rows_count, local_inner)
    gate_act = jax.nn.silu(gate_pre)
    gated_val = mixed_flat * gate_act
    square_total = lax.psum(jnp.sum(gated_val * gated_val, axis=-1), "head")
    scale_back = lax.rsqrt(square_total[:, None] / DI + EPSILON)
    gated_norm = (gated_val * scale_back * gate_gain).astype(jnp.bfloat16)
    branch_part = jnp.dot(gated_norm, output_weight, preferred_element_type=jnp.float32)
    branch = lax.psum_scatter(branch_part, "head", scatter_dimension=1, tiled=True)
    output = (hidden.reshape(rows_count, local_width).astype(jnp.float32) + branch).reshape(
        seq_count, tok_count, local_width
    )
    cot_rows = whole_cotangent.reshape(rows_count, D)
    grad_output_weight = jnp.dot(gated_norm.T, cot_rows, preferred_element_type=jnp.float32)
    grad_norm_out = jnp.dot(cot_rows, output_weight.T, preferred_element_type=jnp.float32)
    grad_gate_gain = jnp.sum(grad_norm_out * gated_val * scale_back, axis=0)
    grad_scaled = grad_norm_out * gate_gain
    dot_total = lax.psum(jnp.sum(grad_scaled * gated_val, axis=-1), "head")
    grad_gated = scale_back * (
        grad_scaled - gated_val * scale_back * scale_back * (dot_total[:, None] / DI)
    )
    grad_mixed = (grad_gated * gate_act).reshape(seq_count, tok_count, heads_local, HEADDIM)
    grad_gate_pre = grad_gated * mixed_flat * silu_slope(gate_pre)
    grad_skip_gain = jnp.sum(grad_mixed * inner_heads, axis=(0, 1, 3))
    from_here = jnp.einsum(
        "sthp,stn->shpn", grad_mixed * jnp.exp(cumlog)[..., None], read_map, precision=HIGH
    )
    suffix_decay, state_grad = entering((total_decay, from_here), "seq", chain_pair, identity, True)
    recomputed, scan_back = jax.vjp(
        batched_scan, inner_heads, write_map, read_map, step_size, decay_rates, state_in
    )
    grad_inner_heads, grad_write, grad_read, grad_step, grad_rates, grad_start = scan_back(
        (grad_mixed, state_grad)
    )
    grad_write, grad_read = lax.psum((grad_write, grad_read), "head")
    grad_maps = jnp.concatenate([grad_write, grad_read], axis=-1)
    grad_inner = (grad_inner_heads + skip_gain[None, None, :, None] * grad_mixed).reshape(
        seq_count, tok_count, local_inner
    )
    grad_inner_conv = grad_inner * silu_slope(inner_conv)
    grad_maps_conv = grad_maps * silu_slope(maps_conv)
    next_inner, next_maps = shifted(
        (grad_inner_conv[:, : CONV - 1, :], grad_maps_conv[:, : CONV - 1, :]), "seq", -1
    )
    inner_ext = jnp.concatenate([grad_inner_conv, next_inner], axis=1)
    maps_ext = jnp.concatenate([grad_maps_conv, next_maps], axis=1)
    grad_inner_pre, grad_inner_kernel, grad_inner_bias = conv_grads(
        inner_pad, inner_ext, grad_inner_conv, inner_kernel, tok_count
    )
    grad_maps_pre, grad_maps_kernel, grad_maps_bias = conv_grads(
        maps_pad, maps_ext, grad_maps_conv, maps_kernel, tok_count
    )
    grad_step_pre = grad_step * jax.nn.sigmoid(step_pre + step_bias)
    grad_step_bias = jnp.sum(grad_step_pre, axis=(0, 1))
    grad_decay_log = grad_rates * decay_rates
    gate_round = grad_gate_pre.astype(jnp.bfloat16)
    inner_round = grad_inner_pre.reshape(rows_count, local_inner).astype(jnp.bfloat16)
    maps_round = grad_maps_pre.reshape(rows_count, 2 * STATE).astype(jnp.bfloat16)
    step_round = grad_step_pre.reshape(rows_count, heads_local).astype(jnp.bfloat16)
    grad_gate_weight = jnp.dot(normed.T, gate_round, preferred_element_type=jnp.float32)
    grad_inner_weight = jnp.dot(normed.T, inner_round, preferred_element_type=jnp.float32)
    grad_maps_weight = jnp.dot(normed.T, maps_round, preferred_element_type=jnp.float32)
    grad_step_weight = jnp.dot(normed.T, step_round, preferred_element_type=jnp.float32)
    partial_normed = jnp.dot(gate_round, gate_weight.T, preferred_element_type=jnp.float32)
    partial_normed = partial_normed + jnp.dot(
        inner_round, inner_weight.T, preferred_element_type=jnp.float32
    )
    partial_normed = partial_normed + jnp.dot(
        step_round, step_weight.T, preferred_element_type=jnp.float32
    )
    input_share = lax.psum_scatter(partial_normed, "head", scatter_dimension=1, tiled=True)
    column_start = lax.axis_index("head") * local_width
    maps_rows = lax.dynamic_slice_in_dim(maps_weight, column_start, local_width, 0)
    input_share = input_share + jnp.dot(maps_round, maps_rows.T, preferred_element_type=jnp.float32)
    normal_local = lax.dynamic_slice_in_dim(normal, column_start, local_width, 1)
    grad_normal = input_share * norm_gain.astype(jnp.float32)
    dot_sum = lax.psum(jnp.sum(grad_normal * normal_local, axis=-1), "head")
    grad_rows = inverse * (grad_normal - normal_local * (dot_sum[:, None] / D)) + cotangent.reshape(
        rows_count, local_width
    ).astype(jnp.float32)
    grad_hidden = grad_rows.reshape(seq_count, tok_count, local_width)
    grad_norm_gain = jnp.sum(input_share * normal_local, axis=0)
    summed = lax.psum(
        (
            grad_norm_gain,
            grad_gate_weight,
            grad_inner_weight,
            grad_step_weight,
            grad_maps_weight,
            grad_inner_kernel,
            grad_inner_bias,
            grad_maps_kernel,
            grad_maps_bias,
            grad_step_bias,
            grad_decay_log,
            grad_skip_gain,
            grad_gate_gain,
            grad_output_weight,
        ),
        ("batch", "seq"),
    )
    return (
        output,
        grad_hidden,
        summed[0],
        summed[1],
        summed[2],
        summed[3],
        summed[4],
        summed[5],
        summed[6],
        summed[7],
        summed[8],
        summed[9],
        summed[10],
        summed[11],
        summed[12],
        summed[13],
    )


def solution(mesh):
    return jax.shard_map(
        on_device,
        mesh=mesh,
        in_specs=(
            P("batch", "seq", "head"),
            P("head"),
            P(None, "head"),
            P(None, "head"),
            P(None, "head"),
            P(),
            P(None, "head"),
            P("head"),
            P(),
            P(),
            P("head"),
            P("head"),
            P("head"),
            P("head"),
            P("head", None),
            P("batch", "seq", "head"),
        ),
        out_specs=(
            P("batch", "seq", "head"),
            P("batch", "seq", "head"),
            P("head"),
            P(None, "head"),
            P(None, "head"),
            P(None, "head"),
            P(),
            P(None, "head"),
            P("head"),
            P(),
            P(),
            P("head"),
            P("head"),
            P("head"),
            P("head"),
            P("head", None),
        ),
        check_vma=False,
    )
```

profile of v0, /device:TPU:0, one launch (start us, length us, event | category | flops | bytes accessed | tf_op | source)
XLA Modules:
  0.0 855.7 jit_solution(2560668838805555344)
XLA Ops:
  13.6 7.7 all-gather.8.cloned.1.call-done
  50.1 70.7 %while.120 = (s32[]{:T(128)}, f32[1,16,64,128]{3,2,1,0:T(8,128)}, f32[2,1,256,16,64]{2,0,4,3,1:T(2,128)}, f32[2,1,256,16]{2,0,3,1:T(2,128)}, f32[16]{0:T(128)S(1...) while((s32[]{:T(128)}, f32[1,16,64,128]{3,2,1,0:T(8,128)}, ...), condition=%wide.region_4.5_spmd.clone.clone, body=%wide.region_1.4_spmd.clone.clone.sunk | while | flops 1717903360 | bytes 23170916 | solution.py:71
  53.6 4.8 fusion.317
  59.5 21.9 %dynamic_update_slice.235 = f32[2,1,256,16,64]{2,0,4,3,1:T(2,128)} dynamic-update-slice(f32[2,1,256,16,64]{2,0,4,3,1:T(2,128)} %get-tuple-element.2732, f32[1,1,256,16,64]{2,0,4,3,1:T(1,128)S(1)} %copy.413, s32[]{:T(128)} %get-tuple-element.2730, s32[]{:T(128)} %constant.258.clone.1..sunk.3, s32[]{:T(128)} %constant.258.clone.1..sunk.3, s32[]{:T(128)} %constant.258.clone.1..sunk.3, ...) | dynamic-update-slice | bytes 2097156 | tf_op jit(solution)/shard_map/vmap()/while/body/jit(dynamic_update_index_in_dim)/dynamic_update_slice | solution.py:71
  89.4 4.8 fusion.317
  95.3 21.9 %dynamic_update_slice.235 = f32[2,1,256,16,64]{2,0,4,3,1:T(2,128)} dynamic-update-slice(f32[2,1,256,16,64]{2,0,4,3,1:T(2,128)} %get-tuple-element.2732, f32[1,1,256,16,64]{2,0,4,3,1:T(1,128)S(1)} %copy.413, s32[]{:T(128)} %get-tuple-element.2730, s32[]{:T(128)} %constant.258.clone.1..sunk.3, s32[]{:T(128)} %constant.258.clone.1..sunk.3, s32[]{:T(128)} %constant.258.clone.1..sunk.3, ...) | dynamic-update-slice | bytes 2097156 | tf_op jit(solution)/shard_map/vmap()/while/body/jit(dynamic_update_index_in_dim)/dynamic_update_slice | solution.py:71
  124.2 9.4 %all_gather.29 = f32[4,1,16]{2,1,0:T(1,128)S(1)} all-gather(f32[1,1,16]{2,1,0:T(1,128)S(1)} %exp.133), channel_id=1, replica_groups=mesh['batch'=4,'seq'=4,'head'=2] {'seq'}, dimensions={0}, use_global_device_ids=true | all-gather | bytes 320 | tf_op jit(solution)/shard_map/all_gather | solution.py:26
  141.9 24.1 %all-gather.12.cloned.1.call-done = f32[4,16,64,128]{3,2,1,0:T(8,128)} async-done(((f32[1,16,64,128]{3,2,1,0:T(8,128)}), f32[4,16,64,128]{3,2,1,0:T(8,128)}) %all-gather.12.cloned.1.call-update) | async-done | bytes 2097168 | tf_op jit(solution)/shard_map/all_gather | solution.py:26
  166.0 4.8 while.118
  180.4 5.5 multiply_reduce_fusion.6
  188.5 5.9 multiply_reduce_fusion
  196.8 6.6 fusion.168
  220.1 46.4 %while.117 = (s32[]{:T(128)}, f32[1,16,64,128]{3,2,1,0:T(8,128)S(1)}, f32[2,1,256,256,16]{3,4,2,1,0:T(8,128)}, f32[2,1,128,256]{2,3,1,0:T(8,128)}, f32[2,1,256,1...) while((s32[]{:T(128)}, ...), condition=%wide.region_19.20_spmd.clone.clone, body=%wide.region_16.19_spmd.clone.clone.sunk | while | flops 912007232 | bytes 91645848 | solution.py:71
  225.2 6.3 multiply_dynamic-update-slice_fusion.4
  248.4 6.3 multiply_dynamic-update-slice_fusion.4
  271.0 4.5 copy.251
  275.5 7.3 while.119
  286.5 108.7 %while.121 = (s32[]{:T(128)}, f32[16]{0:T(128)}, f32[1,16,64,128]{3,2,1,0:T(8,128)S(1)}, f32[2,1,256,16,64]{2,4,3,1,0:T(8,128)}, f32[2,1,256,128]{3,2,1,0:T(8,12...) while((s32[]{:T(128)}, f32[16]{0:T(128)}, ...), condition=%wide.region_32.33_spmd.clone.clone, body=%wide.region_20.32_spmd.clone.clone.sunk | while | flops 3434913792 | bytes 128363696 | solution.py:71
  286.7 6.7 constant_dynamic-slice_fusion.20
  295.7 11.3 %fusion.331 = (f32[256,16]{0,1:T(8,128)}, f32[256,16]{0,1:T(8,128)}, f32[256,256]{1,0:T(8,128)S(1)}) fusion(f32[1,1,256,256,16]{3,4,2,1,0:T(8,128)S(1)} %constant_dynamic-slice_fusion.23, f32[256,256]{1,0:T(8,128)S(1)} %dynamic-slice_bitcast_fusion.8, pred[256,256]{1,0:T(8,128)(4,1)S(1)} %get-tuple-element.2976, ...), kind=kOutput, calls=%fused_computation.161.clone.1 | convolution fusion | flops 813621248 | bytes 11109376 | tf_op jit(solution)/shard_map/transpose(jvp(vmap()))/while/body/eval_jaxpr/tsh,shp->thp/dot_general | solution.py:63
  317.5 8.9 %fusion.330 = (f32[256,16]{0,1:T(8,128)S(1)}, f32[1,256,16,64]{1,3,2,0:T(8,128)}) fusion(f32[2,1,256,16,64]{2,4,3,1,0:T(8,128)} %get-tuple-element.2974, s32[]{:T(128)S(6)} %sub.235, f32[1,1,256,256,16]{3,4,2,1,0:T(8,128)} %get-tuple-element.2704, f32[2,1,256,16,64]{2,4,3,1,0:T(8,128)} %get-tuple-element.2960, ...), kind=kOutput, calls=%fused_computation.139.clone.1 | convolution fusion | flops 806350848 | bytes 8422400 | tf_op jit(solution)/shard_map/transpose(jvp(vmap()))/while/body/eval_jaxpr/tsh,shp->thp/dot_general | solution.py:63
  340.8 6.7 constant_dynamic-slice_fusion.20
  349.9 11.3 %fusion.331 = (f32[256,16]{0,1:T(8,128)}, f32[256,16]{0,1:T(8,128)}, f32[256,256]{1,0:T(8,128)S(1)}) fusion(f32[1,1,256,256,16]{3,4,2,1,0:T(8,128)S(1)} %constant_dynamic-slice_fusion.23, f32[256,256]{1,0:T(8,128)S(1)} %dynamic-slice_bitcast_fusion.8, pred[256,256]{1,0:T(8,128)(4,1)S(1)} %get-tuple-element.2976, ...), kind=kOutput, calls=%fused_computation.161.clone.1 | convolution fusion | flops 813621248 | bytes 11109376 | tf_op jit(solution)/shard_map/transpose(jvp(vmap()))/while/body/eval_jaxpr/tsh,shp->thp/dot_general | solution.py:63
  371.6 8.9 %fusion.330 = (f32[256,16]{0,1:T(8,128)S(1)}, f32[1,256,16,64]{1,3,2,0:T(8,128)}) fusion(f32[2,1,256,16,64]{2,4,3,1,0:T(8,128)} %get-tuple-element.2974, s32[]{:T(128)S(6)} %sub.235, f32[1,1,256,256,16]{3,4,2,1,0:T(8,128)} %get-tuple-element.2704, f32[2,1,256,16,64]{2,4,3,1,0:T(8,128)} %get-tuple-element.2960, ...), kind=kOutput, calls=%fused_computation.139.clone.1 | convolution fusion | flops 806350848 | bytes 8422400 | tf_op jit(solution)/shard_map/transpose(jvp(vmap()))/while/body/eval_jaxpr/tsh,shp->thp/dot_general | solution.py:63
  395.2 4.9 fusion.214
  404.0 4.9 copy.266
  408.8 4.9 reshape.1301
  413.8 6.4 fusion.222
  431.7 4.8 fusion.218
  462.0 81.9 %all-reduce.2 = (f32[512]{0:T(512)}, f32[4,1024]{1,0:T(4,128)}, f32[1024]{0:T(1024)}, f32[4,256]{1,0:T(4,128)}, f32[256]{0:T(256)}, /*index=5*/f32[16]{0:T(128)}, f32[16]{0:T(128)}, f32[16]{0:T(128)}, f32[1024]{0:T(1024)}) all-reduce(f32[512]{0:T(512)S(1)} %get-tuple-element.1965, ...), channel_id=1, replica_groups=mesh['batch'=4,'seq'=4,'head'=2] {'batch','seq'}, use_global_device_ids=true, to_apply=%region_39.40 | all-reduce | flops 7984 | bytes 63872 | tf_op jit(solution)/shard_map/psum | solution.py:263
  546.9 290.1 %all-reduce.8.cloned.1.call-done = (f32[1024,1024]{1,0:T(8,128)}, f32[1024,1024]{1,0:T(8,128)}, f32[1024,16]{0,1:T(8,128)}, f32[1024,256]{1,0:T(8,128)}, f32[1024,1024]{1,0:T(8,128)}) async-done(((f32[1024,1024]{1,0:T(8,128)}, f32[1024,1024]{1,0:T(8,128)}, f32[1024,16]{0,1:T(8,128)}, f32[1024,256]{1,0:T(8,128)}, f32[1024,1024]{1,0:T(8,128)}), (f32[1024,1024]{1,0:T(8,128)}, f32[1024,1024]{1,0:T(8,128)}, ...) | async-done | bytes 13697040 | tf_op jit(solution)/shard_map/psum | solution.py:263
  837.0 4.9 copy.557
  (611 shorter events, 252.2 us)
Async XLA Ops:
  7.2 173.2 %copy-start = (bf16[1024,1024]{1,0:T(8,128)(2,1)S(1)}, bf16[1024,1024]{1,0:T(8,128)(2,1)}, u32[]{:S(2)}) copy-start(bf16[1024,1024]{1,0:T(8,128)(2,1)} %param.28) | copy-start | bytes 6291460
  7.2 14.1 %all-gather.8.cloned.1.call-start = ((), (), s32[]{:S(2)}) async-start(), calls=%async_computation.2 | async-start | bytes 1572864 | tf_op jit(solution)/shard_map/all_gather | solution.py:134
  7.9 158.0 %all-gather.12.cloned.1.call-start = ((), (), s32[]{:S(2)}) async-start(), calls=%async_computation.6 | async-start | bytes 2621440 | tf_op jit(solution)/shard_map/all_gather | solution.py:26
  10.7 169.8 %copy-start.55 = (f32[2,1,512]{2,1,0:T(1,128)}, f32[2,1,512]{2,1,0:T(1,128)S(1)}, u32[]{:S(2)}) copy-start(f32[2,1,512]{2,1,0:T(1,128)S(1)} %convert_element_type.86) | copy-start | bytes 12292
  12.7 23.3 %copy-start.85 = (f32[1,256]{1,0:T(1,128)}, f32[1,256]{1,0:T(1,128)S(1)}, u32[]{:S(2)}) copy-start(f32[1,256]{1,0:T(1,128)S(1)} %get-tuple-element.2197) | copy-start | bytes 3076
  12.7 23.3 %copy-start.87 = (f32[1,256]{1,0:T(1,128)}, f32[1,256]{1,0:T(1,128)S(1)}, u32[]{:S(2)}) copy-start(f32[1,256]{1,0:T(1,128)S(1)} %get-tuple-element.2198) | copy-start | bytes 3076
  12.7 23.3 %copy-start.89 = (f32[1,256]{1,0:T(1,128)}, f32[1,256]{1,0:T(1,128)S(1)}, u32[]{:S(2)}) copy-start(f32[1,256]{1,0:T(1,128)S(1)} %get-tuple-element.2199) | copy-start | bytes 3076
  12.7 23.3 %copy-start.91 = (f32[1,256]{1,0:T(1,128)}, f32[1,256]{1,0:T(1,128)S(1)}, u32[]{:S(2)}) copy-start(f32[1,256]{1,0:T(1,128)S(1)} %get-tuple-element.2200) | copy-start | bytes 3076
  13.6 23.6 %copy-start.68 = (f32[1,1024]{1,0:T(1,128)}, f32[1,1024]{1,0:T(1,128)S(1)}, u32[]{:S(2)}) copy-start(f32[1,1024]{1,0:T(1,128)S(1)} %get-tuple-element.2193) | copy-start | bytes 12292
  13.6 23.6 %copy-start.70 = (f32[1,1024]{1,0:T(1,128)}, f32[1,1024]{1,0:T(1,128)S(1)}, u32[]{:S(2)}) copy-start(f32[1,1024]{1,0:T(1,128)S(1)} %get-tuple-element.2194) | copy-start | bytes 12292
  13.6 23.6 %copy-start.72 = (f32[1,1024]{1,0:T(1,128)}, f32[1,1024]{1,0:T(1,128)S(1)}, u32[]{:S(2)}) copy-start(f32[1,1024]{1,0:T(1,128)S(1)} %get-tuple-element.2195) | copy-start | bytes 12292
  13.6 23.6 %copy-start.74 = (f32[1,1024]{1,0:T(1,128)}, f32[1,1024]{1,0:T(1,128)S(1)}, u32[]{:S(2)}) copy-start(f32[1,1024]{1,0:T(1,128)S(1)} %get-tuple-element.2196) | copy-start | bytes 12292
  23.0 157.4 %copy-start.63 = (f32[512]{0:T(512)}, f32[512]{0:T(512)S(1)}, u32[]{:S(2)}) copy-start(f32[512]{0:T(512)S(1)} %add_rsqrt_fusion.1) | copy-start | bytes 6148
  24.9 11.1 %copy-start.30 = (f32[512,256]{1,0:T(8,128)}, f32[512,256]{1,0:T(8,128)S(1)}, u32[]{:S(2)}) copy-start(f32[512,256]{1,0:T(8,128)S(1)} %fusion.220) | copy-start | bytes 1572868
  24.9 9.9 %copy-start.76 = (bf16[1024,16]{0,1:T(8,128)(2,1)S(1)}, bf16[1024,16]{0,1:T(8,128)(2,1)}, u32[]{:S(2)}) copy-start(bf16[1024,16]{0,1:T(8,128)(2,1)} %param.30) | copy-start | bytes 98308
  24.9 9.9 %copy-start.100 = (f32[16]{0:T(128)S(1)}, f32[16]{0:T(128)}, u32[]{:S(2)}) copy-start(f32[16]{0:T(128)} %param.36) | copy-start | bytes 196
  24.9 11.0 %collective-permute-start.1 = (f32[1,3,256]{2,1,0:T(4,128)S(1)}, f32[1,3,256]{2,1,0:T(4,128)S(1)}, u32[]{:S(2)}, u32[]{:S(2)}) collective-permute-start(f32[1,3,256]{2,1,0:T(4,128)S(1)} %slice.201), channel_id=1, source_target_pairs={{0,2},{2,4},{4,6},{1,3},{3,5},{5,7},{8,10},{10,12},{12,14},{9,11},... | collective-permute-start | bytes 9224 | tf_op jit(solution)/shard_map/ppermute | solution.py:21
  31.4 5.8 collective-permute-start
  120.8 67.6 %all-gather.10.cloned.1.call-start = ((), (), s32[]{:S(2)}) async-start(), calls=%async_computation.4 | async-start | bytes 1572864 | tf_op jit(solution)/shard_map/all_gather | solution.py:135
  121.6 154.0 %all-gather.14.cloned.1.call-start = ((), (), s32[]{:S(2)}) async-start(), calls=%async_computation.7 | async-start | bytes 2621440 | tf_op jit(solution)/shard_map/all_gather | solution.py:26
  180.4 8.0 copy-start.61
  188.4 8.4 copy-start.78
  213.6 227.5 %all-reduce.10.cloned.1.call-start = ((), (), s32[]{:S(2)}) async-start(), calls=%async_computation.9 | async-start | bytes 1048576 | tf_op jit(solution)/shard_map/psum | solution.py:215
  317.5 13.2 %copy-start.57 = (f32[2,1,256,16,1]{2,0,4,3,1:T(2,128)S(1)}, f32[2,1,256,16,1]{2,0,4,3,1:T(2,128)}, u32[]{:S(2)}) copy-start(f32[2,1,256,16,1]{2,0,4,3,1:T(2,128)} %get-tuple-element.2966) | copy-start | bytes 98308 | tf_op jit(solution)/shard_map/transpose(jvp(vmap()))/while
  371.6 13.2 %copy-start.57 = (f32[2,1,256,16,1]{2,0,4,3,1:T(2,128)S(1)}, f32[2,1,256,16,1]{2,0,4,3,1:T(2,128)}, u32[]{:S(2)}) copy-start(f32[2,1,256,16,1]{2,0,4,3,1:T(2,128)} %get-tuple-element.2966) | copy-start | bytes 98308 | tf_op jit(solution)/shard_map/transpose(jvp(vmap()))/while
  395.2 58.2 %reduce-scatter.3.cloned.1.call-start = ((), (), s32[]{:S(2)}) async-start(), calls=%async_computation.3 | async-start | bytes 3145728 | tf_op jit(solution)/shard_map/reduce_scatter | solution.py:189
  400.2 55.8 %reduce-scatter.5.cloned.1.call-start = ((), (), s32[]{:S(2)}) async-start(), calls=%async_computation.5 | async-start | bytes 3145728 | tf_op jit(solution)/shard_map/reduce_scatter | solution.py:251
  413.8 8.0 copy-start.77
  420.3 5.6 collective-permute-start.2
  430.5 406.5 %all-reduce.8.cloned.1.call-start = ((), (), s32[]{:S(2)}) async-start(), calls=%async_computation.8 | async-start | bytes 27394048 | tf_op jit(solution)/shard_map/psum | solution.py:263
  443.6 5.5 collective-permute-start.3
  455.9 88.0 %copy-start.35 = (f32[512,512]{1,0:T(8,128)S(1)}, f32[512,512]{1,0:T(8,128)}, u32[]{:S(2)}) copy-start(f32[512,512]{1,0:T(8,128)} %reduce-scatter.5.cloned.1.call-done) | copy-start | bytes 3145732
  (124 other events, 505.1 us)
Sparse Core Ops, SparseCore 0:
  9.5 11.7 all-gather.7
  121.0 44.9 all-gather.11
  167.5 7.8 all-gather.9
  213.7 44.5 all-gather.13
  395.3 17.5 all-reduce.9
  415.0 10.8 reduce-scatter.2
  430.6 8.5 reduce-scatter.4
  451.1 385.9 all-reduce.7
where the time goes:
time: 872 us; the launch traced here: 856 us
  waiting for transfers between devices  328 us (38%)
  local copies, waits for them, and re-layouts  169 us (19%)
  matrix products  141 us (16%)
  blocking collectives  101 us (12%)
  other arithmetic  90.1 us (10%)
  between operations  15.5 us (2%)
  starting transfers between devices  10.8 us (1%)
    psum x1, waiting for transfers between devices, on_device(): lax.psum((grad_norm_gain, grad_gate_weight, grad_inner_weight, grad_step_...  290 us
    psum x1, blocking collectives, on_device(): lax.psum((grad_norm_gain, grad_gate_weight, grad_inner_weight, grad_step_...  81.9 us
    dynamic_update_slice x24, local copies, waits for them, and re-layouts, ssd_blocks(): lax.scan(advance, initial, (inner_blocks, write_blocks, read_blocks, step...  63.8 us
    dot_general x6, matrix products, advance(): jnp.einsum('tsh,shp->thp', decays * scores[:, :, None], weighted, precisi...  50 us
    unnamed x150, local copies, waits for them, and re-layouts  26.9 us
    all_gather x2, waiting for transfers between devices, entering(): everything = jax.tree.map(lambda part: lax.all_gather(part, axis), array)  24.1 us
    dynamic_slice x18, local copies, waits for them, and re-layouts, ssd_blocks(): lax.scan(advance, initial, (inner_blocks, write_blocks, read_blocks, step...  17.4 us
  transfers between devices with their start and end apart: 12, of which 5 were waited for; matrix products, arithmetic and copies ran while one was open for 18% of the time, Pallas kernels for 0%

commit v1 on v0

v1 whole, which is shorter than its diff:
```python
import jax
import jax.numpy as jnp
from jax import lax
from jax.experimental import pallas as pl
from jax.experimental.pallas import tpu as pltpu
from jax.sharding import PartitionSpec as P

HEADDIM = 64
BLK = 256
PAD = 8
EPSILON = 1e-05
HIGH = lax.Precision.HIGHEST
F32 = jnp.float32
BF16 = jnp.bfloat16
FAR = -1e30


def dot(a, b):
    return jnp.dot(a, b, preferred_element_type=F32)


def dot_t(a, b):
    return lax.dot_general(a, b, (((1,), (1,)), ((), ())), preferred_element_type=F32)


def t_dot(a, b):
    return lax.dot_general(a, b, (((0,), (0,)), ((), ())), preferred_element_type=F32)


def fine(a, b, dims):
    return lax.dot_general(a, b, ((dims[:1], dims[1:]), ((), ())), precision=HIGH, preferred_element_type=F32)


def sigmoid(v):
    return 1.0 / (1.0 + jnp.exp(-v))


def silu_slope(v):
    s = sigmoid(v)
    return s * (1.0 + v * (1.0 - s))


def first_half(shape):
    return lax.broadcasted_iota(jnp.int32, shape, 1) < HEADDIM


def lanes(pair, width):
    return jnp.where(first_half((pair.shape[0], width)), pair[:, 0:1], pair[:, 1:2])


def put_pair(ref, values):
    mask = first_half(values.shape)
    ref[0, :, 0:1] = jnp.sum(jnp.where(mask, values, 0.0), axis=1, keepdims=True)
    ref[0, :, 1:2] = jnp.sum(jnp.where(mask, 0.0, values), axis=1, keepdims=True)


def conv_rows(ext_ref, kern_ref, bias_ref, length):
    taps = kern_ref.shape[0]
    total = bias_ref[...]
    for k in range(taps):
        begin = PAD - (taps - 1) + k
        total = total + kern_ref[k : k + 1, :] * ext_ref[begin : begin + length, :]
    return total


def maps_conv_kernel(ext_ref, kern_ref, bias_ref, conv_ref, act_ref):
    conv = conv_rows(ext_ref, kern_ref, bias_ref, conv_ref.shape[0])
    conv_ref[...] = conv
    act_ref[...] = conv * sigmoid(conv)


def enter_kernel(ext_ref, kern_ref, bias_ref, dt_ref, cum_ref, b_ref, conv_ref, act_ref, xdt_ref, state_ref):
    length, width = conv_ref.shape
    conv = conv_rows(ext_ref, kern_ref, bias_ref, length)
    act = conv * sigmoid(conv)
    conv_ref[...] = conv
    act_ref[...] = act
    xdt = act * lanes(dt_ref[0], width)
    xdt_ref[...] = xdt
    cum = cum_ref[0]
    remain = jnp.exp(cum[length - 1 : length, :] - cum)
    state_ref[...] = fine(b_ref[...], xdt * lanes(remain, width), (0, 0))


def within_kernel(c_ref, b_ref, cum_ref, cumt_ref, xdt_ref, y_ref, g_ref):
    length, width = y_ref.shape

    @pl.when(pl.program_id(0) == 0)
    def _():
        g_ref[...] = fine(c_ref[...], b_ref[...], (1, 1))

    cum = cum_ref[0]
    cumt = cumt_ref[0]
    for r in range(0, length, BLK):
        w = r + BLK
        causal = (lax.broadcasted_iota(jnp.int32, (BLK, w), 0) + r) >= lax.broadcasted_iota(
            jnp.int32, (BLK, w), 1
        )
        g = g_ref[r : r + BLK, :w]
        x = xdt_ref[:w, :].astype(BF16)
        parts = []
        for h in range(2):
            diff = cum[r : r + BLK, h : h + 1] - cumt[h : h + 1, :w]
            m = jnp.exp(jnp.where(causal, diff, FAR))
            parts.append(dot((m * g).astype(BF16), x))
        y_ref[r : r + BLK, :] = jnp.where(first_half((BLK, width)), parts[0], parts[1])


def mix_kernel(y_ref, act_ref, gate_ref, gno_ref, c_ref, s_ref, cum_ref, skip_ref, gain_ref, mixed_ref, rows_ref, sq_ref, dt_ref):
    length, width = y_ref.shape
    carried = fine(c_ref[...], s_ref[...], (1, 0)) * lanes(jnp.exp(cum_ref[0]), width)
    mixed = y_ref[...] + carried + skip_ref[...] * act_ref[...]
    mixed_ref[...] = mixed
    gate = gate_ref[...]
    gated = mixed * (gate * sigmoid(gate))
    first = pl.program_id(0) == 0
    square = gated * gated
    inner = gno_ref[...] * gain_ref[...] * gated

    @pl.when(first)
    def _():
        sq_ref[...] = square
        dt_ref[...] = inner

    @pl.when(jnp.logical_not(first))
    def _():
        sq_ref[...] += square
        dt_ref[...] += inner

    @pl.when(pl.program_id(0) == pl.num_programs(0) - 1)
    def _():
        rows_ref[:, 0:1] = jnp.sum(sq_ref[...], axis=1, keepdims=True)
        rows_ref[:, 1:2] = jnp.sum(dt_ref[...], axis=1, keepdims=True)


def gate_back_kernel(mixed_ref, gate_ref, gno_ref, act_ref, gain_ref, c_ref, s_ref, cum_ref, rows_ref,
                     norm_ref, dy_ref, ground_ref, from_ref, dc_ref, ggain_ref, gskip_ref, plus_ref):
    length, width = mixed_ref.shape
    scale = rows_ref[:, 0:1]
    coef = rows_ref[:, 1:2]
    gate = gate_ref[...]
    sig = sigmoid(gate)
    gate_act = gate * sig
    slope = sig * (1.0 + gate * (1.0 - sig))
    mixed = mixed_ref[...]
    gain = gain_ref[...]
    gno = gno_ref[...]
    gated = mixed * gate_act
    scaled = gated * scale
    norm_ref[...] = (scaled * gain).astype(BF16)
    ggain_ref[...] = jnp.sum(gno * scaled, axis=0, keepdims=True)
    grad_gated = scale * (gno * gain) - gated * coef
    dy = grad_gated * gate_act
    dy_ref[...] = dy
    ground_ref[...] = (grad_gated * mixed * slope).astype(BF16)
    gskip_ref[...] = jnp.sum(dy * act_ref[...], axis=0, keepdims=True)
    dye = dy * lanes(jnp.exp(cum_ref[0]), width)
    c = c_ref[...]
    s = s_ref[...]
    from_ref[...] = fine(c, dye, (0, 0))
    put_pair(plus_ref, dye * fine(c, s, (1, 0)))
    dc = fine(dye, s, (1, 1))
    first = pl.program_id(0) == 0

    @pl.when(first)
    def _():
        dc_ref[...] = dc

    @pl.when(jnp.logical_not(first))
    def _():
        dc_ref[...] += dc


def within_back_kernel(c_ref, b_ref, cum_ref, cumt_ref, xdt_ref, dy_ref, dx_ref, plus_ref, minus_ref, db_ref, dc_ref, g_ref, dg_ref):
    length, width = dx_ref.shape

    @pl.when(pl.program_id(0) == 0)
    def _():
        g_ref[...] = fine(b_ref[...], c_ref[...], (1, 1))
        dg_ref[...] = jnp.zeros_like(dg_ref)

    cum = cum_ref[0]
    cumt = cumt_ref[0]
    plus_ref[...] = jnp.zeros_like(plus_ref)
    for r in range(0, length, BLK):
        w = length - r
        causal = lax.broadcasted_iota(jnp.int32, (BLK, w), 0) <= lax.broadcasted_iota(
            jnp.int32, (BLK, w), 1
        )
        g = g_ref[r : r + BLK, r:]
        x = xdt_ref[r : r + BLK, :]
        dy_fine = dy_ref[r:, :]
        dy = dy_fine.astype(BF16)
        half = first_half((BLK, width))
        parts = []
        dg = None
        for h in range(2):
            diff = cumt[h : h + 1, r:] - cum[r : r + BLK, h : h + 1]
            m = jnp.exp(jnp.where(causal, diff, FAR))
            xh = jnp.where(half == (h == 0), x, jnp.zeros_like(x))
            mq = m * fine(xh, dy_fine, (1, 1))
            dg = mq if dg is None else dg + mq
            d = mq * g
            parts.append(dot((m * g).astype(BF16), dy))
            minus_ref[0, r : r + BLK, h : h + 1] = jnp.sum(d, axis=1, keepdims=True)
            plus_ref[0, h : h + 1, r:] += jnp.sum(d, axis=0, keepdims=True)
        dx_ref[r : r + BLK, :] = jnp.where(half, parts[0], parts[1])
        dg_ref[r : r + BLK, r:] += dg

    @pl.when(pl.program_id(0) == pl.num_programs(0) - 1)
    def _():
        dg = dg_ref[...]
        db_ref[...] = fine(dg, c_ref[...], (1, 0))
        dc_ref[...] = fine(dg, b_ref[...], (0, 0))


def leave_back_kernel(dx_ref, ds_ref, b_ref, act_ref, dy_ref, dt_ref, cum_ref, conv_ref, skip_ref, gic_ref, gdt_ref, minus_ref, db_ref):
    length, width = dx_ref.shape
    cum = cum_ref[0]
    remain = lanes(jnp.exp(cum[length - 1 : length, :] - cum), width)
    ds = ds_ref[...]
    bs = fine(b_ref[...], ds, (1, 0)) * remain
    dxd = dx_ref[...] + bs
    act = act_ref[...]
    dt = lanes(dt_ref[0], width)
    xdt = act * dt
    grad_act = dt * dxd + skip_ref[...] * dy_ref[...]
    gic_ref[...] = grad_act * silu_slope(conv_ref[...])
    put_pair(gdt_ref, dxd * act)
    put_pair(minus_ref, xdt * bs)
    db = fine(xdt * remain, ds, (1, 1))
    first = pl.program_id(0) == 0

    @pl.when(first)
    def _():
        db_ref[...] = db

    @pl.when(jnp.logical_not(first))
    def _():
        db_ref[...] += db


def conv_back_kernel(gic_ref, next_ref, ext_ref, kern_ref, round_ref, gkern_ref, gbias_ref, buf_ref):
    length = gic_ref.shape[0]
    taps = kern_ref.shape[0]
    gic = gic_ref[...]
    buf_ref[:length, :] = gic
    buf_ref[length:, :] = next_ref[...]
    total = None
    for k in range(taps):
        at = taps - 1 - k
        term = kern_ref[k : k + 1, :] * buf_ref[at : at + length, :]
        total = term if total is None else total + term
        begin = PAD - (taps - 1) + k
        gkern_ref[k : k + 1, :] = jnp.sum(gic * ext_ref[begin : begin + length, :], axis=0, keepdims=True)
    round_ref[...] = total.astype(BF16)
    gbias_ref[...] = jnp.sum(gic, axis=0, keepdims=True)


def col(rows, width):
    return pl.BlockSpec((rows, width), lambda i: (0, i))


def full(rows, width):
    return pl.BlockSpec((rows, width), lambda i: (0, 0))


def lead(rows, width):
    return pl.BlockSpec((1, rows, width), lambda i: (i, 0, 0))


def out(shape, dtype=F32):
    return jax.ShapeDtypeStruct(shape, dtype)


def call(kernel, steps, ins, outs, shapes, scratch=()):
    return pl.pallas_call(
        kernel,
        grid=(steps,),
        in_specs=ins,
        out_specs=outs,
        out_shape=shapes,
        scratch_shapes=list(scratch),
        compiler_params=pltpu.CompilerParams(
            dimension_semantics=("arbitrary",), vmem_limit_bytes=48 * 1024 * 1024
        ),
    )


def swap(array):
    count = lax.axis_size("head")
    return lax.ppermute(array, "head", [(i, (i + 1) % count) for i in range(count)])


def shifted(array, by):
    count = lax.axis_size("seq")
    pairs = [(i, i + by) for i in range(count) if 0 <= i + by < count]
    return lax.ppermute(array, "seq", pairs)


def joined(own, other, axis):
    first = lax.axis_index("head") == 0
    low = jnp.where(first, own, other)
    high = jnp.where(first, other, own)
    return jnp.concatenate([low, high], axis=axis)


def entering(state, log_totals, repeat, reverse):
    count, index = lax.axis_size("seq"), lax.axis_index("seq")
    total = None
    log_scale = jnp.zeros_like(log_totals[0])
    for by in range(1, count):
        part = shifted(state, -by if reverse else by).astype(F32)
        term = part * repeat(jnp.exp(log_scale))
        total = term if total is None else total + term
        at = jnp.clip(index + by if reverse else index - by, 0, count - 1)
        log_scale = log_scale + lax.dynamic_index_in_dim(log_totals, at, 0, keepdims=False)
    return total


def on_device(hidden, norm_gain, gate_weight, inner_weight, step_weight, maps_weight, inner_kernel, inner_bias,
              maps_kernel, maps_bias, step_bias, decay_log, skip_gain, gate_gain, output_weight, cotangent):
    seq_count, length, local_width = hidden.shape
    width_all = gate_weight.shape[0]
    inner = gate_weight.shape[1]
    inner_all = inner * lax.axis_size("head")
    heads = step_weight.shape[1]
    state = maps_weight.shape[1] // 2
    pairs = heads // 2
    pw = 2 * HEADDIM
    taps = inner_kernel.shape[0]
    own_h = hidden.reshape(length, local_width)
    own_c = cotangent.reshape(length, local_width)
    heads_n, seq_n = lax.axis_size("head"), lax.axis_size("seq")
    tail = own_h[length - PAD :, :]
    perm = [(s * heads_n + h, (s + 1) * heads_n + (1 - h)) for s in range(seq_n - 1) for h in range(heads_n)]
    tail_own = shifted(tail, 1)
    tail_other = lax.ppermute(tail, ("seq", "head"), perm)
    other_h, other_gain, other_c = swap(own_h), swap(norm_gain), swap(own_c)
    ext_h = joined(
        jnp.concatenate([tail_own, own_h], axis=0), jnp.concatenate([tail_other, other_h], axis=0), 1
    )
    gain = joined(norm_gain, other_gain, 0).astype(F32)
    cot = joined(own_c, other_c, 1)
    residual = ext_h.astype(F32)
    inverse_ext = lax.rsqrt(jnp.mean(residual * residual, axis=-1, keepdims=True) + EPSILON)
    normed_ext = (residual * inverse_ext * gain).astype(BF16)
    normed = normed_ext[PAD:]
    inverse = inverse_ext[PAD:]
    step_pre = dot(normed, step_weight) + step_bias
    maps_ext = dot(normed_ext, maps_weight)
    inner_ext = dot(normed_ext, inner_weight)
    dt = jax.nn.softplus(step_pre)
    rates = -jnp.exp(decay_log)
    lower = (jnp.arange(length)[:, None] >= jnp.arange(length)[None, :]).astype(F32)
    cum = jnp.dot(lower, dt * rates, precision=HIGH)
    log_totals = lax.all_gather(cum[length - 1], "seq")
    pair_of = lambda v: v.reshape(length, pairs, 2).transpose(1, 0, 2)
    unpair = lambda v: v.transpose(1, 0, 2).reshape(length, heads)
    repeat = lambda v: jnp.repeat(v, HEADDIM)[None, :]
    dt_p, cum_p = pair_of(dt), pair_of(cum)
    cumt_p = cum.T.reshape(pairs, 2, length)
    skip_row = repeat(skip_gain)
    gain_row = gate_gain[None, :]

    maps_conv, maps_act = call(
        maps_conv_kernel, 2,
        [col(length + PAD, state), col(taps, state), col(1, state)],
        [col(length, state), col(length, state)],
        [out((length, 2 * state)), out((length, 2 * state))],
    )(maps_ext, maps_kernel, maps_bias[None, :])
    write_map, read_map = maps_act[:, :state], maps_act[:, state:]
    maps_full = full(length, state)
    inner_conv, inner_act, xdt, local_state = call(
        enter_kernel, pairs,
        [col(length + PAD, pw), col(taps, pw), col(1, pw), lead(length, 2), lead(length, 2), maps_full],
        [col(length, pw), col(length, pw), col(length, pw), col(state, pw)],
        [out((length, inner)), out((length, inner)), out((length, inner)), out((state, inner))],
    )(inner_ext, inner_kernel, inner_bias[None, :], dt_p, cum_p, write_map)
    state_in = entering(local_state.astype(BF16), log_totals, repeat, False)
    gate_pre = dot(normed, gate_weight)
    grad_norm_out = dot_t(cot, output_weight)
    within = call(
        within_kernel, pairs,
        [maps_full, maps_full, lead(length, 2), lead(2, length), col(length, pw)],
        col(length, pw), out((length, inner)),
        [pltpu.VMEM((length, length), F32)],
    )(read_map, write_map, cum_p, cumt_p, xdt)
    mixed, row_sums = call(
        mix_kernel, pairs,
        [col(length, pw)] * 4 + [maps_full, col(state, pw), lead(length, 2), col(1, pw), col(1, pw)],
        [col(length, pw), full(length, 2)],
        [out((length, inner)), out((length, 2))],
        [pltpu.VMEM((length, pw), F32), pltpu.VMEM((length, pw), F32)],
    )(within, inner_act, gate_pre, grad_norm_out, read_map, state_in, cum_p, skip_row, gain_row)
    row_sums = row_sums + swap(row_sums)
    scale = lax.rsqrt(row_sums[:, 0:1] / inner_all + EPSILON)
    coef = scale * scale * scale * (row_sums[:, 1:2] / inner_all)
    scales = jnp.concatenate([scale, coef], axis=1)
    gated_norm, grad_mixed, gate_round, from_here, grad_read_in, gate_gain_row, skip_lanes, plus_in = call(
        gate_back_kernel, pairs,
        [col(length, pw)] * 4 + [col(1, pw), maps_full, col(state, pw), lead(length, 2), full(length, 2)],
        [col(length, pw)] * 3 + [col(state, pw), maps_full, col(1, pw), col(1, pw), lead(length, 2)],
        [out((length, inner), BF16), out((length, inner)), out((length, inner), BF16), out((state, inner)),
         out((length, state)), out((1, inner)), out((1, inner)), out((pairs, length, 2))],
    )(mixed, gate_pre, grad_norm_out, inner_act, gain_row, read_map, state_in, cum_p, scales)
    state_grad = entering(from_here.astype(BF16), log_totals, repeat, True)
    reduce = lambda v: lax.psum(v, ("batch", "seq"))
    out_sum = reduce(t_dot(gated_norm, cot).astype(BF16))
    gate_part, out_sum = lax.optimization_barrier((t_dot(normed, gate_round).astype(BF16), out_sum))
    gate_sum = reduce(gate_part)
    grad_output_weight = out_sum.astype(F32)
    dx, plus_w, minus_w, grad_write, grad_read = call(
        within_back_kernel, pairs,
        [maps_full, maps_full, lead(length, 2), lead(2, length), col(length, pw), col(length, pw)],
        [col(length, pw), lead(2, length), lead(length, 2), maps_full, maps_full],
        [out((length, inner)), out((pairs, 2, length)), out((pairs, length, 2)),
         out((length, state)), out((length, state))],
        [pltpu.VMEM((length, length), F32), pltpu.VMEM((length, length), F32)],
    )(read_map, write_map, cum_p, cumt_p, xdt, grad_mixed)
    grad_inner_conv, grad_dt, minus_in, grad_write_in = call(
        leave_back_kernel, pairs,
        [col(length, pw), col(state, pw), maps_full, col(length, pw), col(length, pw), lead(length, 2),
         lead(length, 2), col(length, pw), col(1, pw)],
        [col(length, pw), lead(length, 2), lead(length, 2), maps_full],
        [out((length, inner)), out((pairs, length, 2)), out((pairs, length, 2)), out((length, state))],
    )(dx, state_grad, write_map, inner_act, grad_mixed, dt_p, cum_p, inner_conv, skip_row)
    grad_maps = jnp.concatenate([grad_write + grad_write_in, grad_read + grad_read_in], axis=1)
    grad_maps = grad_maps + swap(grad_maps)
    grad_maps_conv = grad_maps * silu_slope(maps_conv)
    next_inner = shifted(grad_inner_conv[:PAD], -1)
    next_maps = shifted(grad_maps_conv[:PAD], -1)

    def conv_back(gic, nxt, ext, kern, width):
        total = gic.shape[1]
        return call(
            conv_back_kernel, total // width,
            [col(length, width), col(PAD, width), col(length + PAD, width), col(taps, width)],
            [col(length, width), col(taps, width), col(1, width)],
            [out((length, total), BF16), out((taps, total)), out((1, total))],
            [pltpu.VMEM((length + PAD, width), F32)],
        )(gic, nxt, ext, kern)

    inner_round, grad_inner_kernel, grad_inner_bias = conv_back(grad_inner_conv, next_inner, inner_ext, inner_kernel, pw)
    maps_round, grad_maps_kernel, grad_maps_bias = conv_back(grad_maps_conv, next_maps, maps_ext, maps_kernel, state)

    state_out = jnp.exp(repeat(cum[length - 1])) * state_in + local_state
    at_end = jnp.sum(jnp.sum(state_grad * state_out, axis=0).reshape(heads, HEADDIM), axis=1)
    grad_cum = plus_w.reshape(heads, length).T - unpair(minus_w - plus_in + minus_in)
    grad_log = jnp.dot(lower.T, grad_cum, precision=HIGH) + at_end
    grad_step_pre = (unpair(grad_dt) + grad_log * rates) * jax.nn.sigmoid(step_pre)
    grad_decay_log = jnp.sum(grad_log * dt, axis=0) * rates
    grad_step_bias = jnp.sum(grad_step_pre, axis=0)
    grad_skip_gain = jnp.sum(skip_lanes.reshape(heads, HEADDIM), axis=1)
    step_round = grad_step_pre.astype(BF16)

    grad_inner_weight = t_dot(normed, inner_round)
    grad_maps_weight = t_dot(maps_round, normed)
    grad_step_weight = t_dot(step_round, normed)
    inner_part, gate_sum = lax.optimization_barrier((grad_inner_weight.astype(BF16), gate_sum))
    inner_sum = reduce(inner_part)
    grad_gate_weight = gate_sum.astype(F32)

    partial = dot_t(gate_round, gate_weight) + dot_t(inner_round, inner_weight) + dot_t(step_round, step_weight)
    column = lax.axis_index("head") * local_width
    other_column = local_width - column
    own_part = lax.dynamic_slice_in_dim(partial, column, local_width, 1)
    other_part = lax.dynamic_slice_in_dim(partial, other_column, local_width, 1)
    input_share = own_part + swap(other_part.astype(BF16)).astype(F32)
    maps_rows = lax.dynamic_slice_in_dim(maps_weight, column, local_width, 0)
    input_share = input_share + dot_t(maps_round, maps_rows)
    normal_own = own_h.astype(F32) * inverse
    grad_normal = input_share * norm_gain.astype(F32)
    dot_sum = jnp.sum(grad_normal * normal_own, axis=-1, keepdims=True)
    dot_sum = dot_sum + swap(dot_sum)
    grad_hidden = inverse * (grad_normal - normal_own * (dot_sum / width_all)) + own_c.astype(F32)
    grad_norm_gain = jnp.sum(input_share * normal_own, axis=0)

    branch = dot(gated_norm, output_weight)
    own_branch = lax.dynamic_slice_in_dim(branch, column, local_width, 1)
    other_branch = lax.dynamic_slice_in_dim(branch, other_column, local_width, 1)
    output = own_h.astype(F32) + own_branch + swap(other_branch.astype(BF16)).astype(F32)

    misc = [grad_norm_gain, grad_maps_kernel.reshape(-1), grad_maps_bias[0], grad_step_bias, grad_decay_log, grad_skip_gain]
    used = sum(v.shape[0] for v in misc)
    misc_rows = -(-used // inner)
    misc.append(jnp.zeros((misc_rows * inner - used,), F32))
    small_rows = jnp.concatenate(
        [grad_maps_weight.reshape(-1, inner), grad_step_weight.reshape(-1, inner), grad_inner_kernel, grad_inner_bias, gate_gain_row,
         jnp.concatenate(misc).reshape(misc_rows, inner)], axis=0
    )
    small = reduce(small_rows)
    maps_end = 2 * state * width_all // inner
    weight_rows = maps_end + heads * width_all // inner
    at = weight_rows + taps
    tail_flat = small[at + 2 :].reshape(-1)
    ends = [0]
    for v in misc[:-1]:
        ends.append(ends[-1] + v.shape[0])
    tails = [tail_flat[ends[i] : ends[i + 1]] for i in range(len(misc) - 1)]
    shape = (seq_count, length, local_width)
    return (
        output.reshape(shape), grad_hidden.reshape(shape), tails[0], grad_gate_weight, inner_sum.astype(F32),
        small[maps_end:weight_rows].reshape(heads, width_all).T,
        small[:maps_end].reshape(2 * state, width_all).T, small[weight_rows:at], small[at],
        tails[1].reshape(maps_kernel.shape), tails[2], tails[3], tails[4], tails[5], small[at + 1], grad_output_weight,
    )


def solution(mesh):
    rows = P("batch", "seq", "head")
    cols = P(None, "head")
    vec = P("head")
    return jax.shard_map(
        on_device,
        mesh=mesh,
        in_specs=(rows, vec, cols, cols, cols, P(), cols, vec, P(), P(), vec, vec, vec, vec, P("head", None), rows),
        out_specs=(rows, rows, vec, cols, cols, cols, P(), cols, vec, P(), P(), vec, vec, vec, vec, P("head", None)),
        check_vma=False,
    )
```

time: 872 us -> 666 us (0.76); the launches traced: 856 us -> 664 us
  local copies, waits for them, and re-layouts: 169 us -> 48.4 us
  matrix products: 141 us -> 34.2 us
  waiting for transfers between devices: 328 us -> 417 us
  blocking collectives: 101 us -> 17.8 us
  Pallas kernels: 0 us -> 74.5 us
  other arithmetic: 90.1 us -> 32.4 us
  starting transfers between devices: 10.8 us -> 24.8 us
    psum x2 -> x4, waiting for transfers between devices: 290 us -> 407 us  [on_device(): reduce = lambda v: lax.psum(v, ('batch', 'seq'))]
    dot_general x47 -> x17, matrix products: 141 us -> 34.2 us  [the longest x5 11.9 us: dot(): return jnp.dot(a, b, preferred_element_type=F32)]
    psum x4 -> x0, blocking collectives: 89.2 us -> none  [the longest x1 81.9 us: on_device(): lax.psum((grad_norm_gain, grad_gate_weight, grad_inner_weight, grad_step_...]
    pallas_call x0 -> x9, Pallas kernels: none -> 74.5 us  [the longest x1 19.2 us: on_device(): call(within_back_kernel, pairs, [maps_full, maps_full, lead(length, 2), l...]
    dynamic_update_slice x24 -> x0, local copies, waits for them, and re-layouts: 63.8 us -> none  [ssd_blocks(): lax.scan(advance, initial, (inner_blocks, write_blocks, read_blocks, step...]
    all_gather x4 -> x0, waiting for transfers between devices: 31.8 us -> none  [the longest x2 24.1 us: entering(): everything = jax.tree.map(lambda part: lax.all_gather(part, axis), array)]
    another operation x51 -> x1, local copies, waits for them, and re-layouts: 20 us -> 0.08 us  [on_device(): repeat = lambda v: jnp.repeat(v, HEADDIM)[None, :]]
    reduce_sum x11 -> x3, other arithmetic: 21.9 us -> 2.25 us  [the longest x1 1.51 us: on_device(): jnp.sum(state_grad * state_out, axis=0).reshape(heads, HEADDIM)]
  transfers between devices with their start and end apart: 12 -> 22, of which waited for: 5 -> 8; matrix products, arithmetic and copies ran while one was open for 18% -> 13% of each run, Pallas kernels for 0% -> 8%
where the time goes in v1:
time: 666 us; the launch traced here: 664 us
  waiting for transfers between devices  417 us (63%)
  Pallas kernels  74.5 us (11%)
  local copies, waits for them, and re-layouts  48.4 us (7%)
  matrix products  34.2 us (5%)
  other arithmetic  32.4 us (5%)
  starting transfers between devices  24.8 us (4%)
  blocking collectives  17.8 us (3%)
  between operations  14.5 us (2%)
    psum x4, waiting for transfers between devices, on_device(): reduce = lambda v: lax.psum(v, ('batch', 'seq'))  407 us
    unnamed x112, local copies, waits for them, and re-layouts  20.5 us
    pallas_call x1, Pallas kernels, on_device(): call(within_back_kernel, pairs, [maps_full, maps_full, lead(length, 2), l...  19.2 us
    ppermute x9, starting transfers between devices, shifted(): return lax.ppermute(array, 'seq', pairs)  18.5 us
    all_gather x1, blocking collectives, on_device(): log_totals = lax.all_gather(cum[length - 1], 'seq')  17.8 us
    pallas_call x1, Pallas kernels, on_device(): call(gate_back_kernel, pairs, [col(length, pw)] * 4 + [col(1, pw), maps_f...  14.5 us
  transfers between devices with their start and end apart: 22, of which 8 were waited for; matrix products, arithmetic and copies ran while one was open for 13% of the time, Pallas kernels for 8%

profile of v1, /device:TPU:0, one launch (start us, length us, event | category | flops | bytes accessed | tf_op | source)
XLA Modules:
  0.0 663.6 jit_solution(14231096172077151262)
XLA Ops:
  8.1 4.4 collective-permute-start.1
  12.5 3.5 collective-permute-start
  26.6 3.8 fusion.53.ext_ref
  32.5 9.8 %shard_map.280 = (f32[512,1024]{1,0:T(8,128)S(1)}, f32[512,1024]{1,0:T(8,128)S(1)}, f32[512,1024]{1,0:T(8,128)}, f32[128,1024]{1,0:T(8,128)S(1)}) custom-call(f32[520,1024]{1,0:T(8,128)} %fusion.53.ext_ref, f32[4,1024]{1,0:T(4,128)S(1)} %copy-done.20, f32[1,1024]{1,0:T(1,128)S(1)} %bitcast.93, f32[8,512,2]{2,1,0:T(8,128)} %bitcast.96, ...), custom_call_target="tpu_custom_call" | custom-call | tf_op jit(solution)/shard_map/pallas_call | solution.py:374
  46.5 3.5 collective-permute-start.7
  52.0 2.5 collective-permute-start.5
  54.7 17.8 %all-gather = f32[4,1,16]{2,1,0:T(1,128)S(1)} all-gather(f32[1,1,16]{2,1,0:T(1,128)S(1)} %bitcast.111), channel_id=1, replica_groups=mesh['batch'=4,'seq'=4,'head'=2] {'seq'}, dimensions={0}, use_global_device_ids=true | all-gather | bytes 320 | tf_op jit(solution)/shard_map/all_gather | solution.py:357
  74.4 7.7 %shard_map.281.y_ref = f32[512,1024]{1,0:T(8,128)S(1)} custom-call(f32[512,128]{1,0:T(8,128)S(1)} %get-tuple-element.185.c_ref, f32[512,128]{1,0:T(8,128)S(1)} %get-tuple-element.184.b_ref, f32[8,512,2]{2,1,0:T(8,128)S(1)} %bitcast.88, f32[8,2,512]{2,1,0:T(2,128)S(1)} %reshape.144.cumt_ref, f32[512,1024]{1,0:T(8,128)} %get-tuple-element.52.xdt_ref), custom_call_target="tpu_custom_call" | custom-call | tf_op jit(solution)/shard_map/pallas_call | solution.py:383
  82.1 2.6 fusion.22.gate_ref
  86.5 2.6 fusion.15.gno_ref
  90.3 7.8 %shard_map.282 = (f32[512,1024]{1,0:T(8,128)S(1)}, f32[512,2]{1,0:T(8,128)S(1)}) custom-call(f32[512,1024]{1,0:T(8,128)S(1)} %shard_map.281.y_ref, f32[512,1024]{1,0:T(8,128)} %copy-done.2, f32[512,1024]{1,0:T(8,128)} %fusion.22.gate_ref, f32[512,1024]{1,0:T(8,128)} %fusion.15.gno_ref, f32[512,128]{1,0:T(8,128)S(1)} %get-tuple-element.185.c_ref, ...), custom_call_target="tpu_custom_call" | custom-call | tf_op jit(solution)/shard_map/pallas_call | solution.py:389
  100.1 14.5 %shard_map.283 = (bf16[512,1024]{1,0:T(8,128)(2,1)S(1)}, f32[512,1024]{1,0:T(8,128)S(1)}, bf16[512,1024]{1,0:T(8,128)(2,1)S(1)}, f32[128,1024]{1,0:T(8,128)S(1)}...) custom-call(f32[512,1024]{1,0:T(8,128)} %copy-done.14, ...), custom_call_target="tpu_custom_call" | custom-call | tf_op jit(solution)/shard_map/pallas_call | solution.py:400
  119.3 2.6 convolution_convert_fusion
  129.0 19.2 %shard_map.284 = (f32[512,1024]{1,0:T(8,128)S(1)}, f32[8,2,512]{2,1,0:T(2,128)S(1)}, f32[8,512,2]{2,1,0:T(8,128)S(1)}, f32[512,128]{1,0:T(8,128)S(1)}, f32[512,128]{1,0:T(8,128)S(1)}) custom-call(f32[512,128]{1,0:T(8,128)S(1)} %get-tuple-element.185.c_ref, f32[512,128]{1,0:T(8,128)S(1)} %get-tuple-element.184.b_ref, f32[8,512,2]{2,1,0:T(8,128)} %bitcast.86, ...), custom_call_target="tpu_custom_call" | custom-call | tf_op jit(solution)/shard_map/pallas_call | solution.py:413
  155.8 4.7 fusion.55
  160.5 2.7 convolution_convert_fusion.1
  164.8 11.4 %shard_map.285 = (f32[512,1024]{1,0:T(8,128)S(1)}, f32[8,512,2]{2,1,0:T(8,128)S(1)}, f32[8,512,2]{2,1,0:T(8,128)}, f32[512,128]{1,0:T(8,128)S(1)}) custom-call(f32[512,1024]{1,0:T(8,128)} %copy-done.13, f32[128,1024]{1,0:T(8,128)S(1)} %get-tuple-element.173.ds_ref, f32[512,128]{1,0:T(8,128)S(1)} %get-tuple-element.184.b_ref, f32[512,1024]{1,0:T(8,128)} %copy-done.2, ...), custom_call_target="tpu_custom_call" | custom-call | tf_op jit(solution)/shard_map/pallas_call | solution.py:421
  181.2 4.5 add_bitcast_fusion
  188.5 82.2 %all-reduce.7.cloned.1.call-done = bf16[1024,1024]{1,0:T(8,128)(2,1)} async-done(((bf16[1024,1024]{1,0:T(8,128)(2,1)}), bf16[1024,1024]{1,0:T(8,128)(2,1)}) %all-reduce.7.cloned.1.call-update) | async-done | bytes 2097168 | tf_op jit(solution)/shard_map/psum | solution.py:408
  275.6 2.6 collective-permute-done.13.next_ref
  278.2 3.1 shard_map.286
  284.6 4.7 collective-permute-done.16.next_ref
  293.1 4.7 concatenate.39
  297.8 4.6 fusion.54
  302.4 2.6 convolution_convert_fusion.2
  305.1 97.2 %all-reduce.9.cloned.1.call-done = bf16[1024,1024]{1,0:T(8,128)(2,1)} async-done(((bf16[1024,1024]{1,0:T(8,128)(2,1)}), bf16[1024,1024]{1,0:T(8,128)(2,1)}) %all-reduce.9.cloned.1.call-update) | async-done | bytes 2097168 | tf_op jit(solution)/shard_map/psum | solution.py:408
  405.6 3.3 fusion.10
  408.9 112.3 %all-reduce.5.cloned.1.call-done = f32[280,1024]{1,0:T(8,128)} async-done(((f32[280,1024]{1,0:T(8,128)}), f32[280,1024]{1,0:T(8,128)}) %all-reduce.5.cloned.1.call-update) | async-done | bytes 1146896 | tf_op jit(solution)/shard_map/psum | solution.py:408
  531.2 4.5 convert_element_type.105
  535.6 2.5 convert_element_type.103
  538.1 114.9 %all-reduce.11.cloned.1.call-done = bf16[1024,1024]{1,0:T(8,128)(2,1)} async-done(((bf16[1024,1024]{1,0:T(8,128)(2,1)}), bf16[1024,1024]{1,0:T(8,128)(2,1)}) %all-reduce.11.cloned.1.call-update) | async-done | bytes 2097168 | tf_op jit(solution)/shard_map/psum | solution.py:408
  653.0 4.1 convert_element_type.104
  (233 shorter events, 80.4 us)
Async XLA Ops:
  7.2 19.4 %copy-start = (bf16[1024,1024]{1,0:T(8,128)(2,1)S(1)}, bf16[1024,1024]{1,0:T(8,128)(2,1)}, u32[]{:S(2)}) copy-start(bf16[1024,1024]{1,0:T(8,128)(2,1)} %param.19) | copy-start | bytes 6291460
  7.2 263.5 %all-reduce.7.cloned.1.call-start = ((), (), s32[]{:S(2)}) async-start(), calls=%async_computation.1 | async-start | bytes 4194304 | tf_op jit(solution)/shard_map/psum | solution.py:408
  8.1 11.1 %collective-permute-start.1 = (bf16[8,512]{1,0:T(8,128)(2,1)S(1)}, bf16[8,512]{1,0:T(8,128)(2,1)S(1)}, u32[]{:S(2)}, u32[]{:S(2)}) collective-permute-start(bf16[8,512]{1,0:T(8,128)(2,1)S(1)} %slice_bitcast_fusion.2), channel_id=1, source_target_pairs={{0,3},{1,2},{2,5},{3,4},{4,7},{5,6},{8,11},{9,10},{10,13},{11,12},... | collective-permute-start | bytes 24584 | tf_op jit(solution)/shard_map/ppermute | solution.py:338
  12.5 6.8 %collective-permute-start = (bf16[8,512]{1,0:T(8,128)(2,1)S(1)}, bf16[8,512]{1,0:T(8,128)(2,1)S(1)}, u32[]{:S(2)}, u32[]{:S(2)}) collective-permute-start(bf16[8,512]{1,0:T(8,128)(2,1)S(1)} %slice_bitcast_fusion.2), channel_id=1, source_target_pairs={{0,2},{2,4},{4,6},{1,3},{3,5},{5,7},{8,10},{10,12},{12,14},{9,11},... | collective-permute-start | bytes 24584 | tf_op jit(solution)/shard_map/ppermute | solution.py:298
  16.0 3.2 collective-permute-start.2
  16.4 2.0 collective-permute-start.3
  16.5 68.2 %collective-permute-start.4 = (bf16[512,512]{1,0:T(8,128)(2,1)}, bf16[512,512]{1,0:T(8,128)(2,1)}, u32[]{:S(2)}, u32[]{:S(2)}) collective-permute-start(bf16[512,512]{1,0:T(8,128)(2,1)} %bitcast.100), channel_id=1, source_target_pairs={{0,1},{1,0},{2,3},{3,2},{4,5},{5,4},{6,7},{7,6},{8,9},{9,8},{10,11... | collective-permute-start | bytes 1572872 | tf_op jit(solution)/shard_map/ppermute | solution.py:292
  46.5 42.5 %collective-permute-start.7 = (bf16[128,1024]{1,0:T(8,128)(2,1)}, bf16[128,1024]{1,0:T(8,128)(2,1)}, u32[]{:S(2)}, u32[]{:S(2)}) collective-permute-start(bf16[128,1024]{1,0:T(8,128)(2,1)} %convert_element_type.85), channel_id=1, source_target_pairs={{0,6},{1,7},{8,14},{9,15},{16,22},{17,23},{24,30},{25,31}} | collective-permute-start | bytes 786440 | tf_op jit(solution)/shard_map/ppermute | solution.py:298
  50.0 39.0 %collective-permute-start.6 = (bf16[128,1024]{1,0:T(8,128)(2,1)}, bf16[128,1024]{1,0:T(8,128)(2,1)}, u32[]{:S(2)}, u32[]{:S(2)}) collective-permute-start(bf16[128,1024]{1,0:T(8,128)(2,1)} %convert_element_type.85), channel_id=1, source_target_pairs={{0,4},{2,6},{1,5},{3,7},{8,12},{10,14},{9,13},{11,15},{16,20},{18,... | collective-permute-start | bytes 786440 | tf_op jit(solution)/shard_map/ppermute | solution.py:298
  52.0 37.1 %collective-permute-start.5 = (bf16[128,1024]{1,0:T(8,128)(2,1)}, bf16[128,1024]{1,0:T(8,128)(2,1)}, u32[]{:S(2)}, u32[]{:S(2)}) collective-permute-start(bf16[128,1024]{1,0:T(8,128)(2,1)} %convert_element_type.85), channel_id=1, source_target_pairs={{0,2},{2,4},{4,6},{1,3},{3,5},{5,7},{8,10},{10,12},{12,14},{9,11},... | collective-permute-start | bytes 786440 | tf_op jit(solution)/shard_map/ppermute | solution.py:298
  74.4 7.7 %copy-start.29 = (bf16[520,1024]{1,0:T(8,128)(2,1)S(1)}, bf16[520,1024]{1,0:T(8,128)(2,1)}, u32[]{:S(2)}) copy-start(bf16[520,1024]{1,0:T(8,128)(2,1)} %copy-done.28) | copy-start | bytes 3194884
  74.4 7.7 %copy-start.46 = (bf16[1024,1024]{1,0:T(8,128)(2,1)S(1)}, bf16[1024,1024]{1,0:T(8,128)(2,1)}, u32[]{:S(2)}) copy-start(bf16[1024,1024]{1,0:T(8,128)(2,1)} %param.18) | copy-start | bytes 6291460
  98.1 1.6 collective-permute-start.8
  121.9 280.3 %all-reduce.9.cloned.1.call-start = ((), (), s32[]{:S(2)}) async-start(), calls=%async_computation.2 | async-start | bytes 4194304 | tf_op jit(solution)/shard_map/psum | solution.py:408
  124.9 38.4 %collective-permute-start.12 = (bf16[128,1024]{1,0:T(8,128)(2,1)}, bf16[128,1024]{1,0:T(8,128)(2,1)}, u32[]{:S(2)}, u32[]{:S(2)}) collective-permute-start(bf16[128,1024]{1,0:T(8,128)(2,1)} %convert_element_type.91), channel_id=1, source_target_pairs={{6,0},{7,1},{14,8},{15,9},{22,16},{23,17},{30,24},{31,25}} | collective-permute-start | bytes 786440 | tf_op jit(solution)/shard_map/ppermute | solution.py:298
  126.2 37.1 %collective-permute-start.11 = (bf16[128,1024]{1,0:T(8,128)(2,1)}, bf16[128,1024]{1,0:T(8,128)(2,1)}, u32[]{:S(2)}, u32[]{:S(2)}) collective-permute-start(bf16[128,1024]{1,0:T(8,128)(2,1)} %convert_element_type.91), channel_id=1, source_target_pairs={{4,0},{6,2},{5,1},{7,3},{12,8},{14,10},{13,9},{15,11},{20,16},{22,... | collective-permute-start | bytes 786440 | tf_op jit(solution)/shard_map/ppermute | solution.py:298
  127.5 35.8 %collective-permute-start.10 = (bf16[128,1024]{1,0:T(8,128)(2,1)}, bf16[128,1024]{1,0:T(8,128)(2,1)}, u32[]{:S(2)}, u32[]{:S(2)}) collective-permute-start(bf16[128,1024]{1,0:T(8,128)(2,1)} %convert_element_type.91), channel_id=1, source_target_pairs={{2,0},{4,2},{6,4},{3,1},{5,3},{7,5},{10,8},{12,10},{14,12},{11,9},... | collective-permute-start | bytes 786440 | tf_op jit(solution)/shard_map/ppermute | solution.py:298
  270.7 250.5 %all-reduce.5.cloned.1.call-start = ((), (), s32[]{:S(2)}) async-start(), calls=%async_computation | async-start | bytes 2293760 | tf_op jit(solution)/shard_map/psum | solution.py:408
  270.8 7.4 %copy-start.3 = (f32[520,1024]{1,0:T(8,128)S(1)}, f32[520,1024]{1,0:T(8,128)}, u32[]{:S(2)}) copy-start(f32[520,1024]{1,0:T(8,128)} %fusion.53.ext_ref) | copy-start | bytes 6389764
  272.4 5.8 collective-permute-start.13
  275.5 7.4 %collective-permute-start.15 = (f32[512,256]{1,0:T(8,128)S(1)}, f32[512,256]{1,0:T(8,128)S(1)}, u32[]{:S(2)}, u32[]{:S(2)}) collective-permute-start(f32[512,256]{1,0:T(8,128)S(1)} %pad_maximum_fusion.5), channel_id=1, source_target_pairs={{0,1},{1,0},{2,3},{3,2},{4,5},{5,4},{6,7},{7,6},{8,9},{9,8},{10,11... | collective-permute-start | bytes 1572872 | tf_op jit(solution)/shard_map/ppermute | solution.py:292
  282.6 6.6 %copy-start.6 = (f32[520,256]{1,0:T(8,128)S(1)}, f32[520,256]{1,0:T(8,128)}, u32[]{:S(2)}) copy-start(f32[520,256]{1,0:T(8,128)} %copy-done.5) | copy-start | bytes 1597444
  282.7 7.4 %copy-start.31 = (bf16[520,1024]{1,0:T(8,128)(2,1)S(1)}, bf16[520,1024]{1,0:T(8,128)(2,1)}, u32[]{:S(2)}) copy-start(bf16[520,1024]{1,0:T(8,128)(2,1)} %copy-done.28) | copy-start | bytes 3194884
  282.8 8.7 %collective-permute-start.14 = (bf16[512,512]{1,0:T(8,128)(2,1)S(1)}, bf16[512,512]{1,0:T(8,128)(2,1)S(1)}, u32[]{:S(2)}, u32[]{:S(2)}) collective-permute-start(bf16[512,512]{1,0:T(8,128)(2,1)S(1)} %dynamic-slice_convert_fusion), channel_id=1, source_target_pairs={{0,1},{1,0},{2,3},{3,2},{4,5},{5,4},{6,7},{7,6},{8,9},{9,8},{10,11... | collective-permute-start | bytes 1572872 | tf_op jit(solution)/shard_map/ppermute | solution.py:292
  283.1 8.4 %copy-start.33 = (bf16[1,512,512]{2,1,0:T(8,128)(2,1)S(1)}, bf16[1,512,512]{2,1,0:T(8,128)(2,1)}, u32[]{:S(2)}) copy-start(bf16[1,512,512]{2,1,0:T(8,128)(2,1)} %param.16) | copy-start | bytes 1572868
  283.1 8.4 %copy-start.41 = (bf16[1024,256]{1,0:T(8,128)(2,1)S(1)}, bf16[1024,256]{1,0:T(8,128)(2,1)}, u32[]{:S(2)}) copy-start(bf16[1024,256]{1,0:T(8,128)(2,1)} %param.21) | copy-start | bytes 1572868
  283.1 6.2 collective-permute-start.16
  297.8 355.3 %all-reduce.11.cloned.1.call-start = ((), (), s32[]{:S(2)}) async-start(), calls=%async_computation.3 | async-start | bytes 4194304 | tf_op jit(solution)/shard_map/psum | solution.py:408
  305.1 100.5 %copy-start.34 = (bf16[1,512,512]{2,1,0:T(8,128)(2,1)S(1)}, bf16[1,512,512]{2,1,0:T(8,128)(2,1)}, u32[]{:S(2)}) copy-start(bf16[1,512,512]{2,1,0:T(8,128)(2,1)} %param.16) | copy-start | bytes 1572868
  305.1 100.5 %copy-start.38 = (bf16[1,512,512]{2,1,0:T(8,128)(2,1)S(1)}, bf16[1,512,512]{2,1,0:T(8,128)(2,1)}, u32[]{:S(2)}) copy-start(bf16[1,512,512]{2,1,0:T(8,128)(2,1)} %param.31) | copy-start | bytes 1572868
  403.6 2.0 collective-permute-start.9
  403.7 1.9 collective-permute-start.17
  (44 other events, 100.0 us)
Sparse Core Ops, SparseCore 0:
  122.1 148.5 all-reduce.6
  276.2 126.0 all-reduce.8
  408.4 112.7 all-reduce.4
  527.1 125.9 all-reduce.10
